TPU v7x, 128 devices: a whole 4x4x4 slice. The times are simulated.
128 devices in a mesh: grp: 8 (over x_hi, z), mem: 16 (over y, x_lo, core).
Axes of the slice: x: 4 (x_hi: 2, x_lo: 2; x = x_hi * 2 + x_lo), y: 4, z: 4, core: 2. Of those that a mesh axis runs over, the one named last changes fastest.
Arguments:
- candidates: bfloat16 [131072, 4096], P(('grp', 'mem')), may hold values from -1 to 1
- round_one: bfloat16 [8192, 4096], P(('grp', 'mem')), may hold values from -1 to 1
- counts: int32 [8, 16], P('grp', 'mem'), may hold values from 1 to 64, 384 in all within a row
- chosen: int32 [8, 128], P('grp'), may hold values from 0 to 383, as said below
Outputs:
- group_dist: float32 [131072], P(('grp', 'mem'))
- final_dist: float32 [131072], P(('grp', 'mem'))
Inputs may be any that keep to these rules, and one draw needn't show every extreme that they name: In each group the counts sum to 384, and some device of each group has exactly 64. `chosen`: within a group the 128 positions are distinct, each below 384.
All inputs are finite; a program needn't handle non-finite values.
Results may differ from a plain program's by a relative error of at most 0.0003.
Values may be sent and summed in bfloat16 or wider, within the bound.
A program may use at most 128 MiB of HBM per device.

v0:
```python
import jax
import jax.numpy as jnp
from jax import lax
from jax.sharding import PartitionSpec as P


def sq_norms(matrix):
    return jnp.sum(jnp.square(matrix.astype(jnp.float32)), axis=1)


def distances(cand_rows, cand_norm, center_rows):
    inner = lax.dot_general(
        cand_rows, center_rows, (((1,), (1,)), ((), ())), preferred_element_type=jnp.float32
    )
    return cand_norm[:, None] + sq_norms(center_rows)[None, :] - 2.0 * inner


def lookup(table, index_values):
    entries = jnp.arange(table.shape[0], dtype=jnp.int32)
    match = index_values[:, None] == entries[None, :]
    return jnp.sum(jnp.where(match, table[None, :], 0), axis=1)


def body(candidates, round_one, counts, chosen):
    mem_size = lax.axis_size("mem")
    my_index = lax.axis_index("mem")
    slot_max = round_one.shape[0]
    width = round_one.shape[1]
    picks_total = chosen.shape[1]
    group_counts = lax.all_gather(counts, "mem", axis=1, tiled=True)[0]
    offsets = jnp.cumsum(group_counts) - group_counts
    picked_ids = chosen[0]
    cand_norm = sq_norms(candidates)
    start_state = (
        jnp.full((candidates.shape[0],), jnp.inf, jnp.float32),
        jnp.zeros((picks_total, width), jnp.float32),
    )
    block_rows = lax.all_gather(round_one, "mem", axis=0, tiled=True)
    slot_ids = jnp.arange(block_rows.shape[0], dtype=jnp.int32)
    holder = slot_ids // slot_max
    within = slot_ids % slot_max
    usable = within < lookup(group_counts, holder)
    position = lookup(offsets, holder) + within
    gaps = distances(candidates, cand_norm, block_rows)
    gaps = jnp.where(usable[None, :], gaps, jnp.inf)
    nearest = jnp.minimum(start_state[0], jnp.min(gaps, axis=1))
    select = ((picked_ids[:, None] == position[None, :]) & usable[None, :]).astype(jnp.bfloat16)
    collected = jnp.dot(select, block_rows, preferred_element_type=jnp.float32)
    nearest, collected = (nearest, collected)
    picked = collected.astype(jnp.bfloat16)
    final_start = jnp.full((candidates.shape[0],), jnp.inf, jnp.float32)
    share = picks_total // mem_size
    my_share = lax.dynamic_slice_in_dim(picked, my_index * share, share, 0)
    final = jnp.minimum(
        final_start,
        jnp.min(
            distances(
                candidates, cand_norm, lax.all_gather(my_share, ("grp", "mem"), axis=0, tiled=True)
            ),
            axis=1,
        ),
    )
    return (nearest, final)


def solution(mesh):
    in_specs = (P(("grp", "mem"), None), P(("grp", "mem"), None), P("grp", "mem"), P("grp", None))
    out_specs = (P(("grp", "mem")), P(("grp", "mem")))
    return jax.shard_map(body, mesh=mesh, in_specs=in_specs, out_specs=out_specs, check_vma=False)
```

profile of v0, /device:TPU:1, one launch (start us, length us, event | category | flops | bytes accessed | tf_op | source)
XLA Modules:
  0.0 298.8 jit_solution(11337238122814754986)
XLA Ops:
  7.2 0.0 all-gather.3.cloned.1.call-start
  7.2 0.7 all-gather.3.cloned.1.call-update
  7.9 0.0 all-gather.5.cloned.1.call-start
  8.6 1.2 dynamic-slice
  9.8 0.7 bitcast_dynamic-update-slice_fusion
  10.5 11.0 %all-reduce = s32[16]{0:T(128)S(1)} all-reduce(s32[16]{0:T(128)S(1)} %bitcast_dynamic-update-slice_fusion), channel_id=1, replica_groups=mesh['grp'=8,'mem'=16] {'mem'}, use_global_device_ids=true, to_apply=%add | all-reduce | flops 16 | bytes 128
  21.5 0.2 reduce-window_clone.1
  21.7 0.1 select_reduce_fusion.1
  21.8 43.6 %all-gather.3.cloned.1.call-done = bf16[1024,4096]{1,0:T(8,128)(2,1)} async-done(((bf16[64,4096]{1,0:T(8,128)(2,1)}), bf16[1024,4096]{1,0:T(8,128)(2,1)}) %all-gather.3.cloned.1.call-update) | async-done | bytes 8388624 | tf_op jit(solution)/shard_map/all_gather | solution.py:38
  65.5 4.7 %fusion.1 = bf16[128,4096]{1,0:T(8,128)(2,1)S(1)} fusion(bf16[1024,4096]{1,0:T(8,128)(2,1)} %all-gather.3.cloned.1.call-done, s32[1024]{0:T(1024)S(1)} %fusion.10, s32[128]{0:T(128)} %bitcast.17, pred[1024]{0:T(1024)(128)(4,1)S(1)} %fusion.11), kind=kOutput, calls=%fused_computation.6 | convolution fusion | flops 1074003968 | bytes 9442816 | tf_op jit(solution)/shard_map/dot_general | solution.py:48
  70.2 0.6 dynamic-slice_convert_fusion
  70.8 0.0 all-gather.5.cloned.1.call-update
  70.8 0.0 copy-start
  70.8 5.2 %multiply_reduce_fusion.2 = f32[1024]{0:T(1024)S(1)} fusion(bf16[1024,4096]{1,0:T(8,128)(2,1)} %param.4), kind=kLoop, calls=%fused_computation.2 | loop fusion | flops 12581888 | bytes 8392704 | tf_op jit(solution)/shard_map/reduce_sum | solution.py:8
  76.1 0.5 copy-done
  76.6 1.7 multiply_reduce_fusion.1
  78.3 12.3 %select_reduce_fusion = f32[1024]{0:T(1024)} fusion(bf16[1024,4096]{1,0:T(8,128)(2,1)} %param.4, bf16[1024,4096]{1,0:T(8,128)(2,1)S(1)} %copy-done, f32[1024]{0:T(1024)S(1)} %multiply_reduce_fusion.1, f32[1024]{0:T(1024)S(1)} %multiply_reduce_fusion.2, pred[1024]{0:T(1024)(128)(4,1)S(1)} %fusion.11), kind=kOutput, calls=%fused_computation.5 | convolution fusion | flops 8595176448 | bytes 16790528 | tf_op jit(solution)/shard_map/dot_general | solution.py:12
  90.6 183.8 %all-gather.5.cloned.1.call-done = bf16[1024,4096]{1,0:T(8,128)(2,1)} async-done(((bf16[8,4096]{1,0:T(8,128)(2,1)}), bf16[1024,4096]{1,0:T(8,128)(2,1)}) %all-gather.5.cloned.1.call-update) | async-done | bytes 8388624 | tf_op jit(solution)/shard_map/all_gather | solution.py:58
  274.3 0.0 copy-start.1
  274.3 5.2 %multiply_reduce_fusion = f32[1024]{0:T(1024)S(1)} fusion(bf16[1024,4096]{1,0:T(8,128)(2,1)} %all-gather.5.cloned.1.call-done), kind=kLoop, calls=%fused_computation | loop fusion | flops 12581888 | bytes 8392704 | tf_op jit(solution)/shard_map/reduce_sum | solution.py:8
  279.5 0.5 copy-done.1
  280.1 11.9 %fusion = f32[1024]{0:T(1024)} fusion(bf16[1024,4096]{1,0:T(8,128)(2,1)S(1)} %copy-done.1, bf16[1024,4096]{1,0:T(8,128)(2,1)} %param.4, f32[1024]{0:T(1024)S(1)} %multiply_reduce_fusion, f32[1024]{0:T(1024)S(1)} %multiply_reduce_fusion.2), kind=kOutput, calls=%fused_computation.4 | convolution fusion | flops 8594127872 | bytes 16789504 | tf_op jit(solution)/shard_map/dot_general | solution.py:12
  (5 shorter events, 0.0 us)
Async XLA Ops:
  7.2 58.3 %all-gather.3.cloned.1.call-start = ((), (), s32[]{:S(2)}) async-start(), calls=%async_computation | async-start | bytes 8912896 | tf_op jit(solution)/shard_map/all_gather | solution.py:38
  7.9 266.4 %all-gather.5.cloned.1.call-start = ((), (), s32[]{:S(2)}) async-start(), calls=%async_computation.1 | async-start | bytes 8454144 | tf_op jit(solution)/shard_map/all_gather | solution.py:58
  70.8 5.8 %copy-start = (bf16[1024,4096]{1,0:T(8,128)(2,1)S(1)}, bf16[1024,4096]{1,0:T(8,128)(2,1)}, u32[]{:S(2)}) copy-start(bf16[1024,4096]{1,0:T(8,128)(2,1)} %all-gather.3.cloned.1.call-done) | copy-start | bytes 25165828
  274.3 5.8 %copy-start.1 = (bf16[1024,4096]{1,0:T(8,128)(2,1)S(1)}, bf16[1024,4096]{1,0:T(8,128)(2,1)}, u32[]{:S(2)}) copy-start(bf16[1024,4096]{1,0:T(8,128)(2,1)} %all-gather.5.cloned.1.call-done) | copy-start | bytes 25165828
Sparse Core Ops, SparseCore 0:
  9.7 55.7 all-gather.2
  70.9 203.3 all-gather.4
where the time goes:
time: 299 us
  waiting for transfers between devices  228 us (76%)
  matrix products  28.8 us (10%)
  between operations  14.7 us (5%)
  other arithmetic  12.4 us (4%)
  blocking collectives  11 us (4%)
  local copies, waits for them, and re-layouts  3.63 us (1%)
    all_gather x1, waiting for transfers between devices, body(): lax.all_gather(my_share, ('grp', 'mem'), axis=0, tiled=True)  184 us
    all_gather x1, waiting for transfers between devices, body(): block_rows = lax.all_gather(round_one, 'mem', axis=0, tiled=True)  43.6 us
    dot_general x2, matrix products, distances(): lax.dot_general(cand_rows, center_rows, (((1,), (1,)), ((), ())), preferr...  24.1 us
    reduce_sum x3, other arithmetic, sq_norms(): return jnp.sum(jnp.square(matrix.astype(jnp.float32)), axis=1)  12.1 us
    unnamed x1, blocking collectives  11 us
  transfers between devices with their start and end apart: 2, of which 2 were waited for; matrix products, arithmetic and copies ran while one was open for 7% of the time, Pallas kernels for 0%

commit v1 on v0

v1 whole, which is shorter than its diff:
```python
import functools

import jax
import jax.numpy as jnp
from jax import lax
from jax.experimental import pallas as pl
from jax.experimental.pallas import tpu as pltpu
from jax.sharding import PartitionSpec as P

MESH = pl.DeviceIdType.MESH
NT = (((1,), (1,)), ((), ()))
F32 = jnp.float32
BF16 = jnp.bfloat16

ROWS = 1024
WIDTH = 4096
HALF = WIDTH // 2
SLOTS = 64
PICKS = 128
CHIPS = 8
SHARE = PICKS // CHIPS
REST = 32

SHARES = (
    (1, 0, 2, 0, 1024),
    (0, 2, 1, 1024, 1536),
    (1, 2, 0, 1536, 2048),
)


def place():
    g, m = lax.axis_index("grp"), lax.axis_index("mem")
    x = (g // 4) * 2 + (m // 2) % 2
    return x, m // 4, g % 4, m % 2


def device(x, y, z, c):
    return {"grp": (x // 2) * 4 + z, "mem": y * 4 + (x % 2) * 2 + c}


def kernel(
    cand_ref, slot_ref, count_ref, chosen_ref, near_ref, final_ref,
    A, S, CN, M1, M2, R1, R2, FIN, UN, D, NRM, DU, AN,
    local_sem, send_sem, recv_sem,
):
    x, y, z, c = place()
    pos3 = (x, y, z)
    xl = x % 2
    other = 1 - c
    me = lax.axis_index("mem")
    chip = y * 2 + xl
    counter = [0]

    def shifted(dim, o):
        p = list(pos3)
        p[dim] = (p[dim] + o) % 4
        return device(p[0], p[1], p[2], c)

    def in_group(dy, dx, dc):
        return device(x - xl + (xl + dx) % 2, (y + dy) % 4, z, (c + dc) % 2)

    def send(src, dst, dev):
        n = counter[0]
        counter[0] += 1
        cp = pltpu.make_async_remote_copy(
            src_ref=src, dst_ref=dst, send_sem=send_sem.at[n], recv_sem=recv_sem.at[n],
            device_id=dev, device_id_type=MESH,
        )
        cp.start()
        sent.append(cp)
        return cp

    sent = []
    sibling = device(x, y, z, other)

    loads = []
    mine = pltpu.make_async_copy(
        slot_ref.at[:, pl.ds(pl.multiple_of(c * HALF, HALF), HALF)], S.at[c], local_sem.at[0])
    mine.start()
    for h in range(2):
        cp = pltpu.make_async_copy(cand_ref.at[:, h * HALF:(h + 1) * HALF], A.at[h], local_sem.at[1 + h])
        cp.start()
        loads.append(cp)

    group_peers = [(dy, dx, dc) for dy in range(4) for dx in range(2) for dc in range(2) if dy or dx or dc]
    partners = [in_group(*o) for o in group_peers]
    partners += [shifted(2, o) for o in (1, 2, 3)]
    partners += [device((x // 2 * 2 + 2 + i) % 4, y, z, c) for i in (0, 1)]
    barrier = pltpu.get_barrier_semaphore()
    for dev in partners:
        pl.semaphore_signal(barrier, inc=1, device_id=dev, device_id_type=MESH)
    CN[me] = jnp.broadcast_to(count_ref[...], (8, 128))
    pl.semaphore_wait(barrier, len(partners))

    count_copies = [send(CN.at[me], CN.at[me], in_group(*o)) for o in group_peers]
    slot_copy = send(
        slot_ref.at[:, pl.ds(pl.multiple_of(other * HALF, HALF), HALF)], S.at[c], sibling)

    D[...] = jnp.zeros_like(D)
    NRM[...] = jnp.zeros_like(NRM)

    def fold(b):
        b = b.astype(F32)
        b = b * b
        total = b[:, 0:128]
        for k in range(128, b.shape[1], 128):
            total = total + b[:, k:k + 128]
        return total

    for cp in count_copies:
        cp.wait_recv()
    lane = lax.broadcasted_iota(jnp.int32, (1, 128), 1)
    row16 = lax.broadcasted_iota(jnp.int32, (16, 128), 0)
    row128 = lax.broadcasted_iota(jnp.int32, (128, 128), 0)
    cnt = jnp.max(CN[...].astype(F32), axis=1)
    off = jnp.zeros((16, 128), F32)
    for m in range(15):
        off = off + jnp.where(row16 > m, cnt[m:m + 1, :], 0.0)

    def pick(table, index):
        return jnp.sum(jnp.where(row16 == index, table, 0.0), axis=0, keepdims=True)

    chosen_col = jnp.transpose(jnp.broadcast_to(chosen_ref[...].astype(F32), (128, 128)))

    def below(p):
        return jnp.sum(jnp.where(chosen_col < p, 1.0, 0.0), axis=0, keepdims=True)

    def whole(v):
        return v.astype(jnp.int32)

    first_off = pick(off, 2 * chip)
    second = lane >= SLOTS
    within = lane % SLOTS
    start = jnp.where(second, pick(off, 2 * chip + 1), first_off)
    live = jnp.where(second, pick(cnt, 2 * chip + 1), pick(cnt, 2 * chip))
    spot = start + within.astype(F32)
    alive = within.astype(F32) < live
    is_chosen = jnp.sum(jnp.where(chosen_col == spot, 1.0, 0.0), axis=0, keepdims=True) > 0.5
    q, q0 = whole(below(spot)), whole(below(first_off))
    u, u0 = whole(spot) - q, whole(first_off) - q0
    key1 = jnp.where(alive, jnp.where(is_chosen, (q % 8) * 16 + (q - q0) // 8, -1), -1)
    key2 = jnp.where(alive, jnp.where(is_chosen, -1, (u % 8) * 16 + (u - u0) // 8), -1)
    hot1 = jnp.where(row128 == key1, 1.0, 0.0).astype(BF16)
    hot2 = jnp.where(row128 == key2, 1.0, 0.0).astype(BF16)

    mine.wait()
    slot_copy.wait_recv()
    held = S[...].reshape(2 * SLOTS, HALF)
    M1[...] = jnp.dot(hot1, held, preferred_element_type=F32).astype(BF16).reshape(CHIPS, 16, HALF)
    chip_peers = [(dy, dx) for dy in range(4) for dx in range(2) if dy or dx]

    def target(dy, dx):
        return (y + dy) % 4 * 2 + (xl + dx) % 2

    swap1 = [send(M1.at[target(*o)], R1.at[chip], in_group(*o, 0)) for o in chip_peers]
    M2[...] = jnp.dot(hot2, held, preferred_element_type=F32).astype(BF16).reshape(CHIPS, 16, HALF)
    R1[chip] = M1[chip]
    R2[chip] = M2[chip]

    source = lane // 16
    low = jnp.sum(jnp.where(row16 == 2 * source, off, 0.0), axis=0, keepdims=True)
    high = jnp.sum(jnp.where(row16 == 2 * source + 1, off + cnt, 0.0), axis=0, keepdims=True)
    ql, qh = whole(below(low)), whole(below(high))
    ul, uh = whole(low) - ql, whole(high) - qh

    def take(lo, hi, rows):
        at = lo + (chip - lo + 1024) % 8 + 8 * (lane % 16)
        key = jnp.where(at < hi, at // 8, -1)
        rowid = lax.broadcasted_iota(jnp.int32, (rows, 128), 0)
        return jnp.where(rowid == key, 1.0, 0.0).astype(BF16)

    take1, take2 = take(ql, qh, SHARE), take(ul, uh, REST)

    for cp in loads:
        cp.wait()
    for i in range(8):
        rows = slice(i * 128, (i + 1) * 128)
        part = fold(A[0, rows, :]) + fold(A[1, rows, :])
        AN[0:1, rows] = jnp.sum(jnp.transpose(part), axis=0, keepdims=True)

    for cp in swap1:
        cp.wait_recv()
    own = jnp.dot(take1, R1[...].reshape(CHIPS * 16, HALF), preferred_element_type=F32)
    FIN[c, x, y, z] = own.astype(BF16)

    def block(share, s1, s2, s3):
        d1, d2, d3, lo, hi = share
        sel = [None] * 3
        sel[d1], sel[d2], sel[d3] = s1, s2, s3
        return (c, *sel, slice(None), slice(lo, hi))

    ALL = slice(None)

    def cast(share, index, dim, o):
        ref = FIN.at[block(share, *index)]
        return send(ref, ref, shifted(dim, o))

    def relay(share, index):
        ref = FIN.at[block(share, *index)]
        return send(ref, ref, sibling)

    def at(share, k, o):
        return (pos3[share[k]] + o) % 4

    n = len(SHARES)
    local = [[] for _ in range(n)]
    first = []
    for s in SHARES:
        here = (at(s, 0, 0), at(s, 1, 0), at(s, 2, 0))
        first.append([cast(s, here, s[0], o) for o in (1, 3, 2)])
    own_ref = FIN.at[c, x, y, z]
    own_relay = send(own_ref, own_ref, sibling)
    swap2 = [send(M2.at[target(*o)], R2.at[chip], in_group(*o, 0)) for o in chip_peers]

    line = [[[] for _ in range(4)] for _ in range(n)]
    seconds = []
    for i, s in enumerate(SHARES):
        for o, cp in zip((1, 3, 2), first[i]):
            cp.wait_recv()
            local[i].append(relay(s, (at(s, 0, -o), at(s, 1, 0), at(s, 2, 0))))
        row = (ALL, at(s, 1, 0), at(s, 2, 0))
        seconds.append([cast(s, row, s[1], o) for o in (1, 3, 2)])
        line[i][0] = [cast(s, row, s[2], 1), cast(s, row, s[2], 3)]

    for cp in swap2:
        cp.wait_recv()
    UN[c, y, xl] = jnp.dot(
        take2, R2[...].reshape(CHIPS * 16, HALF), preferred_element_type=F32).astype(BF16)
    cut = HALF // 2
    left, right = slice(0, cut), slice(cut, HALF)
    un_relay = []

    def un_send(sel, dev):
        ref = UN.at[sel]
        return send(ref, ref, dev)

    un_relay.append(un_send((c, y, xl), sibling))
    un_y = [un_send((c, y, xl, ALL, left), in_group(o, 0, 0)) for o in (1, 3, 2)]
    un_x = un_send((c, y, xl, ALL, right), in_group(0, 1, 0))

    for j, o in enumerate((1, 3, 2)):
        for i, s in enumerate(SHARES):
            seconds[i][j].wait_recv()
            row = (ALL, at(s, 1, -o), at(s, 2, 0))
            line[i][1 + j] = [cast(s, row, s[2], 1), cast(s, row, s[2], 3)]
            local[i].append(relay(s, row))

    un_x.wait_recv()
    un_relay.append(un_send((c, y, 1 - xl, ALL, right), sibling))
    un_xy = [un_send((c, y, ALL, ALL, right), in_group(o, 0, 0)) for o in (1, 3, 2)]
    for o, cp in zip((1, 3, 2), un_y):
        cp.wait_recv()
        un_relay.append(un_send((c, (y + 4 - o) % 4, xl, ALL, left), sibling))
    un_yx = un_send((c, ALL, xl, ALL, left), in_group(0, 1, 0))

    def plane(share, p, rows=None):
        d3, lo, hi = share[2], share[3], share[4]
        sel = [ALL, ALL, ALL]
        sel[d3] = p
        where = tuple(sel) + (ALL,)
        total = D[where + (ALL,)].reshape(256, ROWS)
        norm = NRM[where + (ALL,)].reshape(256, 128)
        for h in range(2):
            b = FIN[(h,) + where + (slice(lo, hi),)].reshape(256, hi - lo)
            total = total + lax.dot_general(b, A[h, :, lo:hi], NT, preferred_element_type=F32)
            norm = norm + fold(b)
        D[where + (ALL,)] = total.reshape(4, 4, 16, ROWS)
        NRM[where + (ALL,)] = norm.reshape(4, 4, 16, 128)

    own_relay.wait_recv()
    for i, s in enumerate(SHARES):
        for cp in local[i]:
            cp.wait_recv()
        plane(s, at(s, 2, 0))

    relays = [[[], []] for _ in range(n)]
    onward = [[[], []] for _ in range(n)]
    for j, o2 in enumerate((0, 1, 3, 2)):
        for i, s in enumerate(SHARES):
            for k, o in enumerate((1, 3)):
                line[i][j][k].wait_recv()
                row = (ALL, at(s, 1, -o2), at(s, 2, -o))
                if (j < 2) == (k == 0):
                    onward[i][k].append((cast(s, row, s[2], o), o2))
                relays[i][k].append(relay(s, row))

    un_yx.wait_recv()
    un_relay.append(un_send((c, ALL, 1 - xl, ALL, left), sibling))
    for o, cp in zip((1, 3, 2), un_xy):
        cp.wait_recv()
        un_relay.append(un_send((c, (y + 4 - o) % 4, ALL, ALL, right), sibling))

    for k, o in enumerate((1, 3)):
        for i, s in enumerate(SHARES):
            for cp in relays[i][k]:
                cp.wait_recv()
            plane(s, at(s, 2, -o))

    last = [[] for _ in range(n)]
    for k, o in enumerate((1, 3)):
        for i, s in enumerate(SHARES):
            for cp, o2 in onward[i][k]:
                cp.wait_recv()
                last[i].append(relay(s, (ALL, at(s, 1, -o2), at(s, 2, 2))))

    for cp in un_relay:
        cp.wait_recv()
    for h in range(2):
        b = UN[h].reshape(256, HALF)
        part = lax.dot_general(b, A[h], NT, preferred_element_type=F32)
        norm = fold(b)
        if h:
            part = part + DU[...]
            norm = norm + un_norm
            norm = jnp.sum(norm, axis=1, keepdims=True)
            near = jnp.min(norm - 2.0 * part, axis=0, keepdims=True)
        else:
            DU[...] = part
            un_norm = norm

    for i, s in enumerate(SHARES):
        for cp in last[i]:
            cp.wait_recv()
        plane(s, at(s, 2, 2))

    def smallest(dots, norms):
        total = jnp.sum(norms.reshape(-1, 128), axis=1, keepdims=True)
        return jnp.min(total - 2.0 * dots.reshape(-1, ROWS), axis=0, keepdims=True)

    best = jnp.full((1, ROWS), jnp.inf, F32)
    for i in range(4):
        best = jnp.minimum(best, smallest(D[i], NRM[i]))
    for i in range(2):
        px = x - xl + i
        near = jnp.minimum(near, smallest(D[px, :, z], NRM[px, :, z]))
    base = AN[0:1, :]
    near_ref[...] = base + near
    final_ref[...] = base + best
    for cp in sent:
        cp.wait_send()


def body(candidates, round_one, counts, chosen):
    copies = 200
    vmem = pltpu.VMEM
    near, final = pl.pallas_call(
        kernel,
        out_shape=(jax.ShapeDtypeStruct((1, ROWS), F32), jax.ShapeDtypeStruct((1, ROWS), F32)),
        in_specs=[
            pl.BlockSpec(memory_space=pl.ANY),
            pl.BlockSpec(memory_space=pl.ANY),
            pl.BlockSpec(memory_space=vmem),
            pl.BlockSpec(memory_space=vmem),
        ],
        out_specs=(pl.BlockSpec(memory_space=vmem), pl.BlockSpec(memory_space=vmem)),
        scratch_shapes=[
            vmem((2, ROWS, HALF), BF16),
            vmem((2, SLOTS, HALF), BF16),
            vmem((16, 8, 128), jnp.int32),
            vmem((CHIPS, 16, HALF), BF16),
            vmem((CHIPS, 16, HALF), BF16),
            vmem((CHIPS, 16, HALF), BF16),
            vmem((CHIPS, 16, HALF), BF16),
            vmem((2, 4, 4, 4, SHARE, HALF), BF16),
            vmem((2, 4, 2, REST, HALF), BF16),
            vmem((4, 4, 4, SHARE, ROWS), F32),
            vmem((4, 4, 4, SHARE, 128), F32),
            vmem((256, ROWS), F32),
            vmem((1, ROWS), F32),
            pltpu.SemaphoreType.DMA((3,)),
            pltpu.SemaphoreType.DMA((copies,)),
            pltpu.SemaphoreType.DMA((copies,)),
        ],
        compiler_params=pltpu.CompilerParams(
            collective_id=0, has_side_effects=True, vmem_limit_bytes=56 << 20),
    )(candidates, round_one, counts, chosen)
    return near.reshape(ROWS), final.reshape(ROWS)


def solution(mesh):
    in_specs = (P(("grp", "mem"), None), P(("grp", "mem"), None), P("grp", "mem"), P("grp", None))
    out_specs = (P(("grp", "mem")), P(("grp", "mem")))
    return jax.shard_map(body, mesh=mesh, in_specs=in_specs, out_specs=out_specs, check_vma=False)
```

time: 299 us -> 67.4 us (0.23)
  waiting for transfers between devices: 228 us -> 0 us
  Pallas kernels: 0 us -> 63.4 us
  matrix products: 28.8 us -> 0 us
  between operations: 14.7 us -> 1.29 us
  other arithmetic: 12.4 us -> 0 us
  blocking collectives: 11 us -> 0 us
    all_gather x2 -> x0, waiting for transfers between devices: 227 us -> none  [the longest x1 184 us: body(): lax.all_gather(my_share, ('grp', 'mem'), axis=0, tiled=True)]
    pallas_call x0 -> x1, Pallas kernels: none -> 63.4 us  [body(): pl.pallas_call(kernel, out_shape=(jax.ShapeDtypeStruct((1, ROWS), F32), j...]
    dot_general x3 -> x0, matrix products: 28.8 us -> none  [the longest x2 24.1 us: distances(): lax.dot_general(cand_rows, center_rows, (((1,), (1,)), ((), ())), preferr...]
    reduce_sum x4 -> x0, other arithmetic: 12.2 us -> none  [the longest x3 12.1 us: sq_norms(): return jnp.sum(jnp.square(matrix.astype(jnp.float32)), axis=1)]
    unnamed x1 -> x0, blocking collectives: 11 us -> none
  transfers between devices with their start and end apart: 2 -> 0, of which waited for: 2 -> 0; matrix products, arithmetic and copies ran while one was open for 7% -> 0% of each run, Pallas kernels for 0% -> 0%
where the time goes in v1:
time: 67.4 us; the launch traced here: 67.2 us
  Pallas kernels  63.4 us (94%)
  local copies, waits for them, and re-layouts  2.53 us (4%)
  between operations  1.29 us (2%)
    pallas_call x1, Pallas kernels, body(): pl.pallas_call(kernel, out_shape=(jax.ShapeDtypeStruct((1, ROWS), F32), j...  63.4 us
    unnamed x2, local copies, waits for them, and re-layouts  2.53 us

profile of v1, /device:TPU:1, one launch (start us, length us, event | category | flops | bytes accessed | tf_op | source)
XLA Modules:
  0.0 67.2 jit_solution(12003612971512021613)
XLA Ops:
  1.3 63.4 %shard_map.59 = (f32[1,1024]{1,0:T(1,128)}, f32[1,1024]{1,0:T(1,128)}) custom-call(bf16[1024,4096]{1,0:T(8,128)(2,1)} %cand_ref.1, bf16[64,4096]{1,0:T(8,128)(2,1)} %slot_ref.1, s32[1,1]{1,0:T(1,128)S(6)} %copy.8.count_ref, s32[1,128]{1,0:T(1,128)} %chosen_ref.1), custom_call_target="tpu_custom_call" | custom-call | tf_op jit(solution)/shard_map/pallas_call | solution.py:346
  64.7 1.3 %copy.9 = f32[1024]{0:T(1024)} copy(f32[1024]{0:T(1024)} %bitcast.3) | data formatting | bytes 8192
  66.0 1.3 %copy.10 = f32[1024]{0:T(1024)} copy(f32[1024]{0:T(1024)} %bitcast.2) | data formatting | bytes 8192

commit v2 on v0

v2 whole, which is shorter than its diff:
```python
import jax
import jax.numpy as jnp
from jax import lax
from jax.experimental import pallas as pl
from jax.experimental.pallas import tpu as pltpu
from jax.sharding import PartitionSpec as P

MESH = pl.DeviceIdType.MESH
NT = (((1,), (1,)), ((), ()))
F32 = jnp.float32
BF16 = jnp.bfloat16
ALL = slice(None)

ROWS = 1024
WIDTH = 4096
HALF = WIDTH // 2
SLOTS = 64
PICKS = 128
CHIPS = 8
SHARE = PICKS // CHIPS
REST = 32
CUT = HALF // 2

SHARES = (
    (1, 0, 2, 0, 896),
    (0, 2, 1, 896, 1408),
    (1, 2, 0, 1408, 2048),
)


def place():
    g, m = lax.axis_index("grp"), lax.axis_index("mem")
    x = (g // 4) * 2 + (m // 2) % 2
    return x, m // 4, g % 4, m % 2


def device(x, y, z, c):
    return {"grp": (x // 2) * 4 + z, "mem": y * 4 + (x % 2) * 2 + c}


def fold(b):
    b = b.astype(F32)
    b = b * b
    total = b[:, 0:128]
    for k in range(128, b.shape[1], 128):
        total = total + b[:, k:k + 128]
    return total


def kernel(
    cand_ref, slot_ref, count_ref, chosen_ref, out_ref,
    A, S, CN, M, R, MO, RO, FIN, UN, D, NRM, DU,
    local_sem, send_sem, recv_sem,
):
    x, y, z, c = place()
    pos3 = (x, y, z)
    xl = x % 2
    other = 1 - c
    me = lax.axis_index("mem")
    chip = y * 2 + xl
    sibling = device(x, y, z, other)
    used = {"send": 0, "recv": 0}

    def fresh(kind):
        used[kind] += 1
        return used[kind] - 1

    def send(src, dst, dev, out, into):
        pltpu.make_async_remote_copy(
            src_ref=src, dst_ref=dst, send_sem=send_sem.at[out], recv_sem=recv_sem.at[into],
            device_id=dev, device_id_type=MESH,
        ).start()

    def span(ref, out, into):
        return pltpu.make_async_remote_copy(
            src_ref=ref, dst_ref=ref, send_sem=send_sem.at[out], recv_sem=recv_sem.at[into],
            device_id=sibling, device_id_type=MESH,
        )

    def arrived(ref, into):
        span(ref, 0, into).wait_recv()

    leaving = []

    def leave(ref, out):
        leaving.append((ref, out))

    def device_at(dim, coord):
        p = list(pos3)
        p[dim] = coord
        return device(p[0], p[1], p[2], c)

    def in_group(dy, dx, dc):
        return device(x - xl + (xl + dx) % 2, (y + dy) % 4, z, (c + dc) % 2)

    partner, outer = x - xl + 1 - xl, (x + 4 - 1 + 2 * xl) % 4

    def neighbours(dim):
        if dim == 0:
            return ((partner, partner), (outer, outer))
        p = pos3[dim]
        return (((p + 1) % 4, (p + 3) % 4), ((p + 3) % 4, (p + 1) % 4))

    def far(dim):
        return (pos3[dim] + 2) % 4

    mine = pltpu.make_async_copy(
        slot_ref.at[:, pl.ds(pl.multiple_of(c * HALF, HALF), HALF)], S.at[c], local_sem.at[0])
    mine.start()
    loads = []
    for h in range(2):
        cp = pltpu.make_async_copy(cand_ref.at[:, h * HALF:(h + 1) * HALF], A.at[h], local_sem.at[1 + h])
        cp.start()
        loads.append(cp)

    group_peers = [(dy, dx, dc) for dy in range(4) for dx in range(2) for dc in range(2) if dy or dx or dc]
    partners = [in_group(*o) for o in group_peers]
    partners += [device_at(2, (z + o) % 4) for o in (1, 2, 3)]
    partners += [device_at(0, outer), device_at(0, far(0))]
    barrier = pltpu.get_barrier_semaphore()
    for dev in partners:
        pl.semaphore_signal(barrier, inc=1, device_id=dev, device_id_type=MESH)
    CN[me] = jnp.broadcast_to(count_ref[...], (8, 128))
    pl.semaphore_wait(barrier, len(partners))

    out_counts, in_counts = fresh("send"), fresh("recv")
    for o in group_peers:
        send(CN.at[me], CN.at[me], in_group(*o), out_counts, in_counts)
    leave(CN.at[0:15], out_counts)
    out_slots, in_slots = fresh("send"), fresh("recv")
    send(
        slot_ref.at[:, pl.ds(pl.multiple_of(other * HALF, HALF), HALF)], S.at[c], sibling,
        out_slots, in_slots)
    leave(S.at[0], out_slots)

    D[...] = jnp.zeros_like(D)
    NRM[...] = jnp.zeros_like(NRM)

    lane = lax.broadcasted_iota(jnp.int32, (1, 128), 1)
    row8 = lax.broadcasted_iota(jnp.int32, (8, 128), 0)
    row16 = lax.broadcasted_iota(jnp.int32, (16, 128), 0)
    row128 = lax.broadcasted_iota(jnp.int32, (128, 128), 0)
    chosen_col = jnp.transpose(jnp.broadcast_to(chosen_ref[...].astype(F32), (128, 128)))

    def below(p):
        return whole(jnp.sum(jnp.where(chosen_col < p, 1.0, 0.0), axis=0, keepdims=True))

    def whole(v):
        return v.astype(jnp.int32)

    def hot(rows, key):
        return jnp.where(rows == key, 1.0, 0.0).astype(BF16)

    arrived(CN.at[0:15], in_counts)
    cnt = jnp.max(CN[...].astype(F32), axis=1)
    off = jnp.zeros((16, 128), F32)
    for m in range(15):
        off = off + jnp.where(row16 > m, cnt[m:m + 1, :], 0.0)
    end = off + cnt

    def pick(table, index):
        return jnp.sum(jnp.where(row16 == index, table, 0.0), axis=0, keepdims=True)

    def amount(lo, hi, goal):
        return (hi - lo - (goal - lo + 1024) % 8 + 7) // 8

    first_off, last_end = pick(off, 2 * chip), pick(end, 2 * chip + 1)
    second = lane >= SLOTS
    within = lane % SLOTS
    spot = jnp.where(second, pick(off, 2 * chip + 1), first_off) + within.astype(F32)
    live = jnp.where(second, pick(cnt, 2 * chip + 1), pick(cnt, 2 * chip))
    alive = within.astype(F32) < live
    is_chosen = jnp.sum(jnp.where(chosen_col == spot, 1.0, 0.0), axis=0, keepdims=True) > 0.5
    q, q0, q1 = below(spot), below(first_off), below(last_end)
    u, u0 = whole(spot) - q, whole(first_off) - q0
    rank, nth = (u - u0) // 8, 15 - (u - u0) // 8
    apart = nth < amount(q0, q1, u % 8)
    key = jnp.where(is_chosen, (q % 8) * 16 + (q - q0) // 8, jnp.where(apart, -1, (u % 8) * 16 + nth))
    key_apart = jnp.where(is_chosen, -1, jnp.where(apart, u % 8, -1))
    hot_main = hot(row128, jnp.where(alive, key, -1))
    hot_apart = hot(row8, jnp.where(alive, key_apart, -1))

    mine.wait()
    arrived(S.at[0], in_slots)
    held = S[...].reshape(2 * SLOTS, HALF)
    M[...] = jnp.dot(hot_main, held, preferred_element_type=F32).astype(BF16).reshape(CHIPS, 16, HALF)
    out_swap, in_swap = fresh("send"), fresh("recv")
    chip_peers = [(dy, dx) for dy in range(4) for dx in range(2) if dy or dx]

    def target(dy, dx):
        return (y + dy) % 4 * 2 + (xl + dx) % 2

    for o in chip_peers:
        send(M.at[target(*o)], R.at[chip], in_group(*o, 0), out_swap, in_swap)
    leave(M.at[0:7], out_swap)
    MO[...] = jnp.dot(hot_apart, held, preferred_element_type=F32).reshape(CHIPS, 1, HALF)
    out_apart, in_apart = fresh("send"), fresh("recv")
    for o in chip_peers:
        send(MO.at[target(*o)], RO.at[chip], in_group(*o, 0), out_apart, in_apart)
    leave(MO.at[0:7], out_apart)
    R[chip] = M[chip]
    RO[chip] = MO[chip]

    def bounds(source):
        low = jnp.sum(jnp.where(row16 == 2 * source, off, 0.0), axis=0, keepdims=True)
        high = jnp.sum(jnp.where(row16 == 2 * source + 1, end, 0.0), axis=0, keepdims=True)
        ql, qh = below(low), below(high)
        return ql, qh, whole(low) - ql, whole(high) - qh

    ql, qh, ul, uh = bounds(lane // 16)
    nth = lane % 16
    at_q = ql + (chip - ql + 1024) % 8 + 8 * nth
    at_u = ul + (chip - ul + 1024) % 8 + 8 * (15 - nth)
    fits = nth >= amount(ql, qh, chip)
    row32 = lax.broadcasted_iota(jnp.int32, (REST, 128), 0)
    take_chosen = hot(row16, jnp.where(at_q < qh, at_q // 8, -1))
    take_rest = hot(row32, jnp.where(fits, jnp.where(at_u < uh, at_u // 8, -1), -1))
    ql, qh, ul, uh = bounds(lane)
    total = amount(ul, uh, chip)
    excess = amount(ql, qh, chip) + total > 16
    at_u = ul + (chip - ul + 1024) % 8 + 8 * (total - 1)
    take_apart = hot(row32, jnp.where(lane < CHIPS, jnp.where(excess, at_u // 8, -1), -1))

    for cp in loads:
        cp.wait()
    for i in range(8):
        rows = slice(i * 128, (i + 1) * 128)
        part = fold(A[0, rows, :]) + fold(A[1, rows, :])
        out_ref[2:3, rows] = jnp.sum(jnp.transpose(part), axis=0, keepdims=True)

    arrived(R.at[0:7], in_swap)
    got = R[...].reshape(CHIPS * 16, HALF)
    FIN[c, x, y, z] = jnp.dot(take_chosen, got, preferred_element_type=F32).astype(BF16)

    def block(share, s1, s2, s3, half=None):
        d1, d2, d3, lo, hi = share
        sel = [None] * 3
        sel[d1], sel[d2], sel[d3] = s1, s2, s3
        return FIN.at[(c if half is None else half, *sel, ALL, slice(lo, hi))]

    def blocks(share, *shape):
        lead = [slice(0, k) for k in shape]
        lead = [0] * (4 - len(lead)) + lead
        return FIN.at[(*lead, ALL, slice(share[3], share[4]))]

    n = len(SHARES)
    own = [tuple(pos3[s[k]] for k in range(3)) for s in SHARES]
    outs = [[fresh("send") for _ in range(3)] for _ in range(n)]
    planes_in = [[fresh("recv") for _ in range(4)] for _ in range(n)]
    for i, s in enumerate(SHARES):
        leave(blocks(s, 2, 3), outs[i][0])
        leave(blocks(s, 2, 4, 3), outs[i][1])
        leave(blocks(s, 2, 4, 4, 3), outs[i][2])
    out_own = fresh("send")

    def cast(i, k, index, coord, into):
        s = SHARES[i]
        ref = block(s, *index)
        send(ref, ref, device_at(s[k], coord), outs[i][k], into)

    def relay(i, k, index, plane):
        ref = block(SHARES[i], *index)
        send(ref, ref, sibling, outs[i][k], planes_in[i][plane])

    first_in = [fresh("recv") for _ in range(n)]
    for i, s in enumerate(SHARES):
        for o in (1, 3, 2):
            cast(i, 0, own[i], (own[i][0] + o) % 4, first_in[i])
        ref = block(s, *own[i])
        send(ref, ref, sibling, out_own, planes_in[i][0])
    leave(FIN.at[0, 0, 0, 0], out_own)

    rest = jnp.dot(take_rest, got, preferred_element_type=F32)
    arrived(RO.at[0:7], in_apart)
    lone = RO[...].reshape(CHIPS, HALF).astype(BF16)
    lone = jnp.concatenate([lone, jnp.zeros((128 - CHIPS, HALF), BF16)], axis=0)
    rest = rest + jnp.dot(take_apart, lone, preferred_element_type=F32)
    UN[c, y, xl] = rest.astype(BF16)
    left, right = slice(0, CUT), slice(CUT, HALF)
    un_in = fresh("recv")
    un_out = fresh("send")
    leave(UN.at[0], un_out)
    outs_y, ins_y = fresh("send"), fresh("recv")
    outs_x, ins_x = fresh("send"), fresh("recv")
    outs_yx, ins_yx = fresh("send"), fresh("recv")
    outs_xy, ins_xy = fresh("send"), fresh("recv")

    def pass_on(sel, dev, out, into):
        ref = UN.at[sel]
        send(ref, ref, dev, out, into)

    for o in (1, 3, 2):
        pass_on((c, y, xl, ALL, left), in_group(o, 0, 0), outs_y, ins_y)
    leave(UN.at[0, 0:3, 0, :, left], outs_y)
    pass_on((c, y, xl, ALL, right), in_group(0, 1, 0), outs_x, ins_x)
    leave(UN.at[0, 0, 0, :, right], outs_x)
    pass_on((c, y, xl), sibling, un_out, un_in)

    line_in = [[[fresh("recv") for _ in range(2)] for _ in range(4)] for _ in range(n)]
    lines = [[None] * 4 for _ in range(n)]
    second_in = [[fresh("recv") for _ in range(3)] for _ in range(n)]

    def third(i, j, coord):
        s = SHARES[i]
        lines[i][j] = coord
        for k, (goal, _) in enumerate(neighbours(s[2])):
            cast(i, 2, (ALL, coord, own[i][2]), goal, line_in[i][j][k])

    for i, s in enumerate(SHARES):
        arrived(blocks(s, 3), first_in[i])
        row = (ALL, own[i][1], own[i][2])
        for k, (goal, _) in enumerate(neighbours(s[1])):
            cast(i, 1, row, goal, second_in[i][k])
        if s[1] != 0:
            cast(i, 1, row, far(s[1]), second_in[i][2])
        third(i, 0, own[i][1])
        for o in (1, 3, 2):
            relay(i, 0, ((own[i][0] + o) % 4, own[i][1], own[i][2]), 0)

    arrived(UN.at[0, 0, 0, :, right], ins_x)
    for o in (1, 3, 2):
        pass_on((c, y, ALL, ALL, right), in_group(o, 0, 0), outs_xy, ins_xy)
    leave(UN.at[0, 0:3, :, :, right], outs_xy)
    pass_on((c, y, 1 - xl, ALL, right), sibling, un_out, un_in)
    arrived(UN.at[0, 0:3, 0, :, left], ins_y)
    pass_on((c, ALL, xl, ALL, left), in_group(0, 1, 0), outs_yx, ins_yx)
    leave(UN.at[0, :, 0, :, left], outs_yx)
    for o in (1, 2, 3):
        pass_on((c, (y + o) % 4, xl, ALL, left), sibling, un_out, un_in)

    for j in range(3):
        for i, s in enumerate(SHARES):
            arrived(blocks(s, 4), second_in[i][j])
            coord = neighbours(s[1])[j][1] if j < 2 else far(s[1])
            row = (ALL, coord, own[i][2])
            if s[1] == 0 and j == 0:
                cast(i, 1, row, outer, second_in[i][2])
            third(i, 1 + j, coord)
            relay(i, 1, row, 0)

    arrived(UN.at[0, :, 0, :, left], ins_yx)
    pass_on((c, ALL, 1 - xl, ALL, left), sibling, un_out, un_in)
    arrived(UN.at[0, 0:3, :, :, right], ins_xy)
    for o in (1, 2, 3):
        pass_on((c, (y + o) % 4, ALL, ALL, right), sibling, un_out, un_in)

    def plane(i, p):
        d3, lo, hi = SHARES[i][2:]
        where = [ALL, ALL, ALL, ALL]
        where[d3] = p
        where = tuple(where)
        total = D[where + (ALL,)].reshape(256, ROWS)
        norm = NRM[where + (ALL,)].reshape(256, 128)
        for h in range(2):
            b = FIN[(h,) + where + (slice(lo, hi),)].reshape(256, hi - lo)
            total = total + lax.dot_general(b, A[h, :, lo:hi], NT, preferred_element_type=F32)
            norm = norm + fold(b)
        D[where + (ALL,)] = total.reshape(4, 4, SHARE, ROWS)
        NRM[where + (ALL,)] = norm.reshape(4, 4, SHARE, 128)

    far_in = [[fresh("recv") for _ in range(4)] for _ in range(n)]
    for j in range(4):
        for i, s in enumerate(SHARES):
            near_by = neighbours(s[2])
            for k, (goal, origin) in enumerate(near_by):
                arrived(blocks(s, 4), line_in[i][j][k])
                row = (ALL, lines[i][j], origin)
                if s[2] == 0:
                    if k == 0:
                        cast(i, 2, row, outer, far_in[i][j])
                elif (j < 2) == (k == 0):
                    cast(i, 2, row, goal, far_in[i][j])
                relay(i, 2, row, 1 + k)
        if j < n:
            arrived(blocks(SHARES[j], 4, 4), planes_in[j][0])
            plane(j, own[j][2])

    arrived(UN.at[0], un_in)
    un_norm = 0.0
    for h in range(2):
        b = UN[h].reshape(256, HALF)
        part = lax.dot_general(b, A[h], NT, preferred_element_type=F32)
        un_norm = un_norm + fold(b)
        if h:
            un_norm = jnp.sum(un_norm, axis=1, keepdims=True)
            out_ref[0:1, :] = jnp.min(un_norm - 2.0 * (DU[...] + part), axis=0, keepdims=True)
        else:
            DU[...] = part

    def far_line(j):
        for i, s in enumerate(SHARES):
            arrived(blocks(s, 4), far_in[i][j])
            relay(i, 2, (ALL, lines[i][j], far(s[2])), 3)

    j = 0
    for k in range(2):
        for i, s in enumerate(SHARES):
            arrived(blocks(s, 4, 4), planes_in[i][1 + k])
            plane(i, neighbours(s[2])[k][1])
            if 1 <= k * n + i <= 4:
                far_line(j)
                j += 1
    for i, s in enumerate(SHARES):
        arrived(blocks(s, 4, 4), planes_in[i][3])
        plane(i, far(s[2]))

    def smallest(dots, norms):
        total = jnp.sum(norms.reshape(-1, 128), axis=1, keepdims=True)
        return jnp.min(total - 2.0 * dots.reshape(-1, ROWS), axis=0, keepdims=True)

    best = jnp.full((1, ROWS), jnp.inf, F32)
    for i in range(4):
        best = jnp.minimum(best, smallest(D[i], NRM[i]))
    near = out_ref[0:1, :]
    for i in range(2):
        px = x - xl + i
        near = jnp.minimum(near, smallest(D[px, :, z], NRM[px, :, z]))
    out_ref[0:1, :] = near
    out_ref[1:2, :] = best
    for ref, out in leaving:
        span(ref, out, 0).wait_send()


def body(candidates, round_one, counts, chosen):
    vmem = pltpu.VMEM
    out = pl.pallas_call(
        kernel,
        out_shape=jax.ShapeDtypeStruct((3, ROWS), F32),
        in_specs=[
            pl.BlockSpec(memory_space=pl.ANY),
            pl.BlockSpec(memory_space=pl.ANY),
            pl.BlockSpec(memory_space=vmem),
            pl.BlockSpec(memory_space=vmem),
        ],
        out_specs=pl.BlockSpec(memory_space=vmem),
        scratch_shapes=[
            vmem((2, ROWS, HALF), BF16),
            vmem((2, SLOTS, HALF), BF16),
            vmem((16, 8, 128), jnp.int32),
            vmem((CHIPS, 16, HALF), BF16),
            vmem((CHIPS, 16, HALF), BF16),
            vmem((CHIPS, 1, HALF), F32),
            vmem((CHIPS, 1, HALF), F32),
            vmem((2, 4, 4, 4, SHARE, HALF), BF16),
            vmem((2, 4, 2, REST, HALF), BF16),
            vmem((4, 4, 4, SHARE, ROWS), F32),
            vmem((4, 4, 4, SHARE, 128), F32),
            vmem((256, ROWS), F32),
            pltpu.SemaphoreType.DMA((3,)),
            pltpu.SemaphoreType.DMA((19,)),
            pltpu.SemaphoreType.DMA((69,)),
        ],
        compiler_params=pltpu.CompilerParams(
            collective_id=0, has_side_effects=True, vmem_limit_bytes=56 << 20),
    )(candidates, round_one, counts, chosen)
    return out[0] + out[2], out[1] + out[2]


def solution(mesh):
    in_specs = (P(("grp", "mem"), None), P(("grp", "mem"), None), P("grp", "mem"), P("grp", None))
    out_specs = (P(("grp", "mem")), P(("grp", "mem")))
    return jax.shard_map(body, mesh=mesh, in_specs=in_specs, out_specs=out_specs, check_vma=False)
```

time: 299 us -> 62.3 us (0.21)
  waiting for transfers between devices: 228 us -> 0 us
  Pallas kernels: 0 us -> 59.3 us
  matrix products: 28.8 us -> 0 us
  between operations: 14.7 us -> 1.28 us
  blocking collectives: 11 us -> 0 us
  other arithmetic: 12.4 us -> 1.44 us
  local copies, waits for them, and re-layouts: 3.63 us -> 0 us
    all_gather x2 -> x0, waiting for transfers between devices: 227 us -> none  [the longest x1 184 us: body(): lax.all_gather(my_share, ('grp', 'mem'), axis=0, tiled=True)]
    pallas_call x0 -> x1, Pallas kernels: none -> 59.3 us  [body(): pl.pallas_call(kernel, out_shape=jax.ShapeDtypeStruct((3, ROWS), F32), in...]
    dot_general x3 -> x0, matrix products: 28.8 us -> none  [the longest x2 24.1 us: distances(): lax.dot_general(cand_rows, center_rows, (((1,), (1,)), ((), ())), preferr...]
    reduce_sum x4 -> x0, other arithmetic: 12.2 us -> none  [the longest x3 12.1 us: sq_norms(): return jnp.sum(jnp.square(matrix.astype(jnp.float32)), axis=1)]
    unnamed x1 -> x0, blocking collectives: 11 us -> none
    unnamed x7 -> x0, local copies, waits for them, and re-layouts: 3 us -> none
  transfers between devices with their start and end apart: 2 -> 0, of which waited for: 2 -> 0; matrix products, arithmetic and copies ran while one was open for 7% -> 0% of each run, Pallas kernels for 0% -> 0%
where the time goes in v2:
time: 62.3 us; the launch traced here: 62.1 us
  Pallas kernels  59.3 us (95%)
  other arithmetic  1.44 us (2%)
  between operations  1.28 us (2%)
    pallas_call x1, Pallas kernels, body(): pl.pallas_call(kernel, out_shape=jax.ShapeDtypeStruct((3, ROWS), F32), in...  59.3 us
    add x1, other arithmetic, body(): return (out[0] + out[2], out[1] + out[2])  1.44 us

profile of v2, /device:TPU:1, one launch (start us, length us, event | category | flops | bytes accessed | tf_op | source)
XLA Modules:
  0.0 62.1 jit_solution(3302292664252524349)
XLA Ops:
  1.3 59.3 %shard_map.59 = f32[3,1024]{1,0:T(4,128)} custom-call(bf16[1024,4096]{1,0:T(8,128)(2,1)} %cand_ref.1, bf16[64,4096]{1,0:T(8,128)(2,1)} %slot_ref.1, s32[1,1]{1,0:T(1,128)S(6)} %copy.6.count_ref, s32[1,128]{1,0:T(1,128)} %chosen_ref.1), custom_call_target="tpu_custom_call" | custom-call | tf_op jit(solution)/shard_map/pallas_call | solution.py:426
  60.6 1.4 %slice_add_fusion = (f32[1,1024]{1,0:T(1,128)}, f32[1,1024]{1,0:T(1,128)}) fusion(f32[3,1024]{1,0:T(4,128)} %shard_map.59), kind=kLoop, calls=%fused_computation | loop fusion | flops 2048 | bytes 20480 | tf_op jit(solution)/shard_map/add | solution.py:456

commit v3 on v2

--- a/solution.py
+++ b/solution.py
@@ -19,12 +19,12 @@
 CHIPS = 8
 SHARE = PICKS // CHIPS
 REST = 32
-CUT = HALF // 2
+CUT = HALF * 3 // 4
 
 SHARES = (
-    (1, 0, 2, 0, 896),
-    (0, 2, 1, 896, 1408),
-    (1, 2, 0, 1408, 2048),
+    (1, 0, 2, 0, 1024),
+    (0, 2, 1, 1024, 1536),
+    (2, 1, 0, 1536, 2048),
 )
 
 
@@ -49,7 +49,7 @@
 
 def kernel(
     cand_ref, slot_ref, count_ref, chosen_ref, out_ref,
-    A, S, CN, M, R, MO, RO, FIN, UN, D, NRM, DU,
+    CT, CH, A, S, CN, M, R, MO, RO, FIN, UN, D, NRM, DU, NU,
     local_sem, send_sem, recv_sem,
 ):
     x, y, z, c = place()
@@ -104,6 +104,19 @@
     def far(dim):
         return (pos3[dim] + 2) % 4
 
+    group_peers = [(dy, dx, dc) for dy in range(4) for dx in range(2) for dc in range(2) if dy or dx or dc]
+    partners = [in_group(*o) for o in group_peers]
+    partners += [device_at(2, (z + o) % 4) for o in (1, 2, 3)]
+    partners += [device_at(0, outer), device_at(0, far(0))]
+    barrier = pltpu.get_barrier_semaphore()
+    for dev in partners:
+        pl.semaphore_signal(barrier, inc=1, device_id=dev, device_id_type=MESH)
+    small = [
+        pltpu.make_async_copy(count_ref, CT, local_sem.at[3]),
+        pltpu.make_async_copy(chosen_ref, CH, local_sem.at[4]),
+    ]
+    for cp in small:
+        cp.start()
     mine = pltpu.make_async_copy(
         slot_ref.at[:, pl.ds(pl.multiple_of(c * HALF, HALF), HALF)], S.at[c], local_sem.at[0])
     mine.start()
@@ -113,14 +126,9 @@
         cp.start()
         loads.append(cp)
 
-    group_peers = [(dy, dx, dc) for dy in range(4) for dx in range(2) for dc in range(2) if dy or dx or dc]
-    partners = [in_group(*o) for o in group_peers]
-    partners += [device_at(2, (z + o) % 4) for o in (1, 2, 3)]
-    partners += [device_at(0, outer), device_at(0, far(0))]
-    barrier = pltpu.get_barrier_semaphore()
-    for dev in partners:
-        pl.semaphore_signal(barrier, inc=1, device_id=dev, device_id_type=MESH)
-    CN[me] = jnp.broadcast_to(count_ref[...], (8, 128))
+    for cp in small:
+        cp.wait()
+    CN[me] = jnp.broadcast_to(CT[...], (8, 128))
     pl.semaphore_wait(barrier, len(partners))
 
     out_counts, in_counts = fresh("send"), fresh("recv")
@@ -140,7 +148,7 @@
     row8 = lax.broadcasted_iota(jnp.int32, (8, 128), 0)
     row16 = lax.broadcasted_iota(jnp.int32, (16, 128), 0)
     row128 = lax.broadcasted_iota(jnp.int32, (128, 128), 0)
-    chosen_col = jnp.transpose(jnp.broadcast_to(chosen_ref[...].astype(F32), (128, 128)))
+    chosen_col = jnp.transpose(jnp.broadcast_to(CH[...].astype(F32), (128, 128)))
 
     def below(p):
         return whole(jnp.sum(jnp.where(chosen_col < p, 1.0, 0.0), axis=0, keepdims=True))
@@ -306,17 +314,106 @@
         for k, (goal, _) in enumerate(neighbours(s[2])):
             cast(i, 2, (ALL, coord, own[i][2]), goal, line_in[i][j][k])
 
-    for i, s in enumerate(SHARES):
+    for i in (1, 2, 0):
+        s = SHARES[i]
         arrived(blocks(s, 3), first_in[i])
         row = (ALL, own[i][1], own[i][2])
         for k, (goal, _) in enumerate(neighbours(s[1])):
             cast(i, 1, row, goal, second_in[i][k])
         if s[1] != 0:
             cast(i, 1, row, far(s[1]), second_in[i][2])
+    for i, s in enumerate(SHARES):
         third(i, 0, own[i][1])
+    for i, s in enumerate(SHARES):
         for o in (1, 3, 2):
             relay(i, 0, ((own[i][0] + o) % 4, own[i][1], own[i][2]), 0)
 
+    def more(j):
+        for i, s in enumerate(SHARES):
+            arrived(blocks(s, 4), second_in[i][j])
+            coord = neighbours(s[1])[j][1] if j < 2 else far(s[1])
+            row = (ALL, coord, own[i][2])
+            if s[1] == 0 and j == 0:
+                cast(i, 1, row, outer, second_in[i][2])
+            third(i, 1 + j, coord)
+            relay(i, 1, row, 0)
+
+    def spread(i, d1, d2, d3):
+        sel = [None] * 3
+        sel[SHARES[i][0]], sel[SHARES[i][1]], sel[SHARES[i][2]] = d1, d2, d3
+        return tuple(sel) + (ALL,)
+
+    def multiply(i, h, parts):
+        lo, hi = SHARES[i][3:]
+        count = 256 // len(parts)
+        rows = [FIN[(h,) + sel + (slice(lo, hi),)].reshape(count, hi - lo) for sel in parts]
+        b = rows[0] if len(rows) == 1 else jnp.concatenate(rows, axis=0)
+        dots = lax.dot_general(b, A[h, :, lo:hi], NT, preferred_element_type=F32)
+        norms = fold(b)
+        for p, sel in enumerate(parts):
+            at = slice(p * count, (p + 1) * count)
+            where = sel + (ALL,)
+            D[where] += dots[at].reshape(D[where].shape)
+            NRM[where] += norms[at].reshape(NRM[where].shape)
+
+    far_in = [[fresh("recv") for _ in range(4)] for _ in range(n)]
+
+    def line(j):
+        for i, s in enumerate(SHARES):
+            for k, (goal, origin) in enumerate(neighbours(s[2])):
+                arrived(blocks(s, 4), line_in[i][j][k])
+                row = (ALL, lines[i][j], origin)
+                if s[2] == 0:
+                    if k == 0:
+                        cast(i, 2, row, outer, far_in[i][j])
+                elif (j < 2) == (k == 0):
+                    cast(i, 2, row, goal, far_in[i][j])
+                relay(i, 2, row, 1 + j // 2)
+
+    def parts(i, k):
+        s = SHARES[i]
+        if k in (0, 3):
+            return [spread(i, ALL, ALL, far(s[2]) if k else own[i][2])]
+        js = (0, 1) if k == 1 else (2, 3)
+        return [spread(i, ALL, lines[i][j], origin) for j in js for _, origin in neighbours(s[2])]
+
+    def own_half(k):
+        for i in (1, 2, 0):
+            multiply(i, c, parts(i, k))
+
+    def other_half(k):
+        for i in (1, 2, 0):
+            arrived(blocks(SHARES[i], 4, 4), planes_in[i][k])
+            multiply(i, other, parts(i, k))
+
+    def far_line(j):
+        for i in (1, 2, 0):
+            s = SHARES[i]
+            arrived(blocks(s, 4), far_in[i][j])
+            relay(i, 2, (ALL, lines[i][j], far(s[2])), 3)
+
+    def un_dots(h):
+        b = UN[h].reshape(256, HALF)
+        return lax.dot_general(b, A[h], NT, preferred_element_type=F32), fold(b)
+
+    def un_own():
+        DU[...], NU[...] = un_dots(c)
+
+    def un_other():
+        arrived(UN.at[0], un_in)
+        dots, norms = un_dots(other)
+        norms = jnp.sum(NU[...] + norms, axis=1, keepdims=True)
+        out_ref[0:1, :] = jnp.min(norms - 2.0 * (DU[...] + dots), axis=0, keepdims=True)
+
+    def un_collect():
+        arrived(UN.at[0, :, 0, :, left], ins_yx)
+        pass_on((c, ALL, 1 - xl, ALL, left), sibling, un_out, un_in)
+        arrived(UN.at[0, 0:3, :, :, right], ins_xy)
+        for o in (1, 2, 3):
+            pass_on((c, (y + o) % 4, ALL, ALL, right), sibling, un_out, un_in)
+
+    more(0)
+    more(1)
     arrived(UN.at[0, 0, 0, :, right], ins_x)
     for o in (1, 3, 2):
         pass_on((c, y, ALL, ALL, right), in_group(o, 0, 0), outs_xy, ins_xy)
@@ -327,82 +424,26 @@
     leave(UN.at[0, :, 0, :, left], outs_yx)
     for o in (1, 2, 3):
         pass_on((c, (y + o) % 4, xl, ALL, left), sibling, un_out, un_in)
-
-    for j in range(3):
-        for i, s in enumerate(SHARES):
-            arrived(blocks(s, 4), second_in[i][j])
-            coord = neighbours(s[1])[j][1] if j < 2 else far(s[1])
-            row = (ALL, coord, own[i][2])
-            if s[1] == 0 and j == 0:
-                cast(i, 1, row, outer, second_in[i][2])
-            third(i, 1 + j, coord)
-            relay(i, 1, row, 0)
-
-    arrived(UN.at[0, :, 0, :, left], ins_yx)
-    pass_on((c, ALL, 1 - xl, ALL, left), sibling, un_out, un_in)
-    arrived(UN.at[0, 0:3, :, :, right], ins_xy)
-    for o in (1, 2, 3):
-        pass_on((c, (y + o) % 4, ALL, ALL, right), sibling, un_out, un_in)
-
-    def plane(i, p):
-        d3, lo, hi = SHARES[i][2:]
-        where = [ALL, ALL, ALL, ALL]
-        where[d3] = p
-        where = tuple(where)
-        total = D[where + (ALL,)].reshape(256, ROWS)
-        norm = NRM[where + (ALL,)].reshape(256, 128)
-        for h in range(2):
-            b = FIN[(h,) + where + (slice(lo, hi),)].reshape(256, hi - lo)
-            total = total + lax.dot_general(b, A[h, :, lo:hi], NT, preferred_element_type=F32)
-            norm = norm + fold(b)
-        D[where + (ALL,)] = total.reshape(4, 4, SHARE, ROWS)
-        NRM[where + (ALL,)] = norm.reshape(4, 4, SHARE, 128)
-
-    far_in = [[fresh("recv") for _ in range(4)] for _ in range(n)]
-    for j in range(4):
-        for i, s in enumerate(SHARES):
-            near_by = neighbours(s[2])
-            for k, (goal, origin) in enumerate(near_by):
-                arrived(blocks(s, 4), line_in[i][j][k])
-                row = (ALL, lines[i][j], origin)
-                if s[2] == 0:
-                    if k == 0:
-                        cast(i, 2, row, outer, far_in[i][j])
-                elif (j < 2) == (k == 0):
-                    cast(i, 2, row, goal, far_in[i][j])
-                relay(i, 2, row, 1 + k)
-        if j < n:
-            arrived(blocks(SHARES[j], 4, 4), planes_in[j][0])
-            plane(j, own[j][2])
-
-    arrived(UN.at[0], un_in)
-    un_norm = 0.0
-    for h in range(2):
-        b = UN[h].reshape(256, HALF)
-        part = lax.dot_general(b, A[h], NT, preferred_element_type=F32)
-        un_norm = un_norm + fold(b)
-        if h:
-            un_norm = jnp.sum(un_norm, axis=1, keepdims=True)
-            out_ref[0:1, :] = jnp.min(un_norm - 2.0 * (DU[...] + part), axis=0, keepdims=True)
-        else:
-            DU[...] = part
-
-    def far_line(j):
-        for i, s in enumerate(SHARES):
-            arrived(blocks(s, 4), far_in[i][j])
-            relay(i, 2, (ALL, lines[i][j], far(s[2])), 3)
-
-    j = 0
-    for k in range(2):
-        for i, s in enumerate(SHARES):
-            arrived(blocks(s, 4, 4), planes_in[i][1 + k])
-            plane(i, neighbours(s[2])[k][1])
-            if 1 <= k * n + i <= 4:
-                far_line(j)
-                j += 1
-    for i, s in enumerate(SHARES):
-        arrived(blocks(s, 4, 4), planes_in[i][3])
-        plane(i, far(s[2]))
+    line(0)
+    more(2)
+    own_half(0)
+    line(1)
+    other_half(0)
+    own_half(1)
+    line(2)
+    other_half(1)
+    far_line(0)
+    line(3)
+    un_collect()
+    un_own()
+    far_line(1)
+    own_half(2)
+    far_line(2)
+    other_half(2)
+    far_line(3)
+    un_other()
+    own_half(3)
+    other_half(3)
 
     def smallest(dots, norms):
         total = jnp.sum(norms.reshape(-1, 128), axis=1, keepdims=True)
@@ -429,11 +470,13 @@
         in_specs=[
             pl.BlockSpec(memory_space=pl.ANY),
             pl.BlockSpec(memory_space=pl.ANY),
-            pl.BlockSpec(memory_space=vmem),
-            pl.BlockSpec(memory_space=vmem),
+            pl.BlockSpec(memory_space=pl.ANY),
+            pl.BlockSpec(memory_space=pl.ANY),
         ],
         out_specs=pl.BlockSpec(memory_space=vmem),
         scratch_shapes=[
+            vmem((1, 1), jnp.int32),
+            vmem((1, PICKS), jnp.int32),
             vmem((2, ROWS, HALF), BF16),
             vmem((2, SLOTS, HALF), BF16),
             vmem((16, 8, 128), jnp.int32),
@@ -446,7 +489,8 @@
             vmem((4, 4, 4, SHARE, ROWS), F32),
             vmem((4, 4, 4, SHARE, 128), F32),
             vmem((256, ROWS), F32),
-            pltpu.SemaphoreType.DMA((3,)),
+            vmem((256, 128), F32),
+            pltpu.SemaphoreType.DMA((5,)),
             pltpu.SemaphoreType.DMA((19,)),
             pltpu.SemaphoreType.DMA((69,)),
         ],

time: 62.3 us -> 57.5 us (0.923)
  Pallas kernels: 59.3 us -> 54.4 us
    pallas_call x1, Pallas kernels: 59.3 us -> 54.4 us  [body(): pl.pallas_call(kernel, out_shape=jax.ShapeDtypeStruct((3, ROWS), F32), in...]
where the time goes in v3:
time: 57.5 us; the launch traced here: 57.1 us
  Pallas kernels  54.4 us (95%)
  other arithmetic  1.44 us (3%)
  between operations  1.28 us (2%)
    pallas_call x1, Pallas kernels, body(): pl.pallas_call(kernel, out_shape=jax.ShapeDtypeStruct((3, ROWS), F32), in...  54.4 us
    add x1, other arithmetic, body(): return (out[0] + out[2], out[1] + out[2])  1.44 us

profile of v3, /device:TPU:1, one launch (start us, length us, event | category | flops | bytes accessed | tf_op | source)
XLA Modules:
  0.0 57.1 jit_solution(5084193893626712210)
XLA Ops:
  1.3 54.4 %shard_map.59 = f32[3,1024]{1,0:T(4,128)} custom-call(bf16[1024,4096]{1,0:T(8,128)(2,1)} %cand_ref.1, bf16[64,4096]{1,0:T(8,128)(2,1)} %slot_ref.1, s32[1,1]{1,0:T(1,128)S(6)} %copy.6.count_ref, s32[1,128]{1,0:T(1,128)} %chosen_ref.1), custom_call_target="tpu_custom_call" | custom-call | tf_op jit(solution)/shard_map/pallas_call | solution.py:467
  55.7 1.4 %slice_add_fusion = (f32[1,1024]{1,0:T(1,128)}, f32[1,1024]{1,0:T(1,128)}) fusion(f32[3,1024]{1,0:T(4,128)} %shard_map.59), kind=kLoop, calls=%fused_computation | loop fusion | flops 2048 | bytes 20480 | tf_op jit(solution)/shard_map/add | solution.py:500

commit v4 on v3

--- a/solution.py
+++ b/solution.py
@@ -21,6 +21,8 @@
 REST = 32
 CUT = HALF * 3 // 4
 
+RING = (0,)
+EARLY = (0,)
 SHARES = (
     (1, 0, 2, 0, 1024),
     (0, 2, 1, 1024, 1536),
@@ -270,10 +272,15 @@
         ref = block(SHARES[i], *index)
         send(ref, ref, sibling, outs[i][k], planes_in[i][plane])
 
+    line_in = [[[fresh("recv") for _ in range(2)] for _ in range(4)] for _ in range(n)]
     first_in = [fresh("recv") for _ in range(n)]
     for i, s in enumerate(SHARES):
         for o in (1, 3, 2):
             cast(i, 0, own[i], (own[i][0] + o) % 4, first_in[i])
+    for i in EARLY:
+        for k, (goal, _) in enumerate(neighbours(SHARES[i][2])):
+            cast(i, 2, own[i], goal, line_in[i][0][k])
+    for i, s in enumerate(SHARES):
         ref = block(s, *own[i])
         send(ref, ref, sibling, out_own, planes_in[i][0])
     leave(FIN.at[0, 0, 0, 0], out_own)
@@ -304,7 +311,6 @@
     leave(UN.at[0, 0, 0, :, right], outs_x)
     pass_on((c, y, xl), sibling, un_out, un_in)
 
-    line_in = [[[fresh("recv") for _ in range(2)] for _ in range(4)] for _ in range(n)]
     lines = [[None] * 4 for _ in range(n)]
     second_in = [[fresh("recv") for _ in range(3)] for _ in range(n)]
 
@@ -320,10 +326,16 @@
         row = (ALL, own[i][1], own[i][2])
         for k, (goal, _) in enumerate(neighbours(s[1])):
             cast(i, 1, row, goal, second_in[i][k])
-        if s[1] != 0:
+        if s[1] not in RING:
             cast(i, 1, row, far(s[1]), second_in[i][2])
     for i, s in enumerate(SHARES):
-        third(i, 0, own[i][1])
+        if i in EARLY:
+            lines[i][0] = own[i][1]
+            for o in (1, 3, 2):
+                for k, (goal, _) in enumerate(neighbours(s[2])):
+                    cast(i, 2, ((own[i][0] + o) % 4, own[i][1], own[i][2]), goal, line_in[i][0][k])
+        else:
+            third(i, 0, own[i][1])
     for i, s in enumerate(SHARES):
         for o in (1, 3, 2):
             relay(i, 0, ((own[i][0] + o) % 4, own[i][1], own[i][2]), 0)
@@ -335,6 +347,9 @@
             row = (ALL, coord, own[i][2])
             if s[1] == 0 and j == 0:
                 cast(i, 1, row, outer, second_in[i][2])
+            elif s[1] in RING and s[1] != 0 and j < 2:
+                half = (slice(2 * j, 2 * j + 2), coord, own[i][2])
+                cast(i, 1, half, neighbours(s[1])[j][0], second_in[i][2])
             third(i, 1 + j, coord)
             relay(i, 1, row, 0)
 
@@ -429,10 +444,10 @@
     own_half(0)
     line(1)
     other_half(0)
+    line(2)
     own_half(1)
-    line(2)
+    far_line(0)
     other_half(1)
-    far_line(0)
     line(3)
     un_collect()
     un_own()

time: 57.5 us -> 57 us (level)
  no operation moved by 1% of the time
where the time goes in v4:
time: 57 us; the launch traced here: 56.6 us
  Pallas kernels  53.9 us (95%)
  other arithmetic  1.44 us (3%)
  between operations  1.28 us (2%)
    pallas_call x1, Pallas kernels, body(): pl.pallas_call(kernel, out_shape=jax.ShapeDtypeStruct((3, ROWS), F32), in...  53.9 us
    add x1, other arithmetic, body(): return (out[0] + out[2], out[1] + out[2])  1.44 us

profile of v4, /device:TPU:1, one launch (start us, length us, event | category | flops | bytes accessed | tf_op | source)
XLA Modules:
  0.0 56.6 jit_solution(7138274333666768369)
XLA Ops:
  1.3 53.9 %shard_map.59 = f32[3,1024]{1,0:T(4,128)} custom-call(bf16[1024,4096]{1,0:T(8,128)(2,1)} %cand_ref.1, bf16[64,4096]{1,0:T(8,128)(2,1)} %slot_ref.1, s32[1,1]{1,0:T(1,128)S(6)} %copy.6.count_ref, s32[1,128]{1,0:T(1,128)} %chosen_ref.1), custom_call_target="tpu_custom_call" | custom-call | tf_op jit(solution)/shard_map/pallas_call | solution.py:482
  55.1 1.4 %slice_add_fusion = (f32[1,1024]{1,0:T(1,128)}, f32[1,1024]{1,0:T(1,128)}) fusion(f32[3,1024]{1,0:T(4,128)} %shard_map.59), kind=kLoop, calls=%fused_computation | loop fusion | flops 2048 | bytes 20480 | tf_op jit(solution)/shard_map/add | solution.py:515

commit v5 on v4

--- a/solution.py
+++ b/solution.py
@@ -272,14 +272,14 @@
         ref = block(SHARES[i], *index)
         send(ref, ref, sibling, outs[i][k], planes_in[i][plane])
 
-    line_in = [[[fresh("recv") for _ in range(2)] for _ in range(4)] for _ in range(n)]
+    line_in = [[fresh("recv") for _ in range(4)] for _ in range(n)]
     first_in = [fresh("recv") for _ in range(n)]
     for i, s in enumerate(SHARES):
         for o in (1, 3, 2):
             cast(i, 0, own[i], (own[i][0] + o) % 4, first_in[i])
     for i in EARLY:
         for k, (goal, _) in enumerate(neighbours(SHARES[i][2])):
-            cast(i, 2, own[i], goal, line_in[i][0][k])
+            cast(i, 2, own[i], goal, line_in[i][0])
     for i, s in enumerate(SHARES):
         ref = block(s, *own[i])
         send(ref, ref, sibling, out_own, planes_in[i][0])
@@ -318,7 +318,7 @@
         s = SHARES[i]
         lines[i][j] = coord
         for k, (goal, _) in enumerate(neighbours(s[2])):
-            cast(i, 2, (ALL, coord, own[i][2]), goal, line_in[i][j][k])
+            cast(i, 2, (ALL, coord, own[i][2]), goal, line_in[i][j])
 
     for i in (1, 2, 0):
         s = SHARES[i]
@@ -333,7 +333,7 @@
             lines[i][0] = own[i][1]
             for o in (1, 3, 2):
                 for k, (goal, _) in enumerate(neighbours(s[2])):
-                    cast(i, 2, ((own[i][0] + o) % 4, own[i][1], own[i][2]), goal, line_in[i][0][k])
+                    cast(i, 2, ((own[i][0] + o) % 4, own[i][1], own[i][2]), goal, line_in[i][0])
         else:
             third(i, 0, own[i][1])
     for i, s in enumerate(SHARES):
@@ -375,8 +375,8 @@
 
     def line(j):
         for i, s in enumerate(SHARES):
+            arrived(blocks(s, 2, 4), line_in[i][j])
             for k, (goal, origin) in enumerate(neighbours(s[2])):
-                arrived(blocks(s, 4), line_in[i][j][k])
                 row = (ALL, lines[i][j], origin)
                 if s[2] == 0:
                     if k == 0:
@@ -507,7 +507,7 @@
             vmem((256, 128), F32),
             pltpu.SemaphoreType.DMA((5,)),
             pltpu.SemaphoreType.DMA((19,)),
-            pltpu.SemaphoreType.DMA((69,)),
+            pltpu.SemaphoreType.DMA((57,)),
         ],
         compiler_params=pltpu.CompilerParams(
             collective_id=0, has_side_effects=True, vmem_limit_bytes=56 << 20),

time: 57 us -> 56.9 us (level)
  no operation moved by 1% of the time
where the time goes in v5:
time: 56.9 us; the launch traced here: 56.5 us
  Pallas kernels  53.8 us (95%)
  other arithmetic  1.44 us (3%)
  between operations  1.28 us (2%)
    pallas_call x1, Pallas kernels, body(): pl.pallas_call(kernel, out_shape=jax.ShapeDtypeStruct((3, ROWS), F32), in...  53.8 us
    add x1, other arithmetic, body(): return (out[0] + out[2], out[1] + out[2])  1.44 us

profile of v5, /device:TPU:1, one launch (start us, length us, event | category | flops | bytes accessed | tf_op | source)
XLA Modules:
  0.0 56.5 jit_solution(10532898078533160687)
XLA Ops:
  1.3 53.8 %shard_map.59 = f32[3,1024]{1,0:T(4,128)} custom-call(bf16[1024,4096]{1,0:T(8,128)(2,1)} %cand_ref.1, bf16[64,4096]{1,0:T(8,128)(2,1)} %slot_ref.1, s32[1,1]{1,0:T(1,128)S(6)} %copy.6.count_ref, s32[1,128]{1,0:T(1,128)} %chosen_ref.1), custom_call_target="tpu_custom_call" | custom-call | tf_op jit(solution)/shard_map/pallas_call | solution.py:482
  55.0 1.4 %slice_add_fusion = (f32[1,1024]{1,0:T(1,128)}, f32[1,1024]{1,0:T(1,128)}) fusion(f32[3,1024]{1,0:T(4,128)} %shard_map.59), kind=kLoop, calls=%fused_computation | loop fusion | flops 2048 | bytes 20480 | tf_op jit(solution)/shard_map/add | solution.py:515
